TPU v7x, 256 devices: a whole 4x4x8 slice. The times are simulated.
256 devices in a mesh: row: 16 (over z, core), col: 16 (over y, x).
Axes of the slice: x: 4, y: 4, z: 8, core: 2. Of those that a mesh axis runs over, the one named last changes fastest.
Arguments:
- right_sides: float32 [4, 1024, 4096], P(None, 'row', 'col'), may hold values from -6 to 6
- low_left: bfloat16 [6, 4096, 128], P(None, 'col'), may hold values from -0.25 to 0.25
- low_right: bfloat16 [6, 4096, 128], P(None, 'col'), may hold values from -0.09375 to 0.09375
- up_left: bfloat16 [6, 4096, 128], P(None, 'col'), may hold values from -0.25 to 0.25
- up_right: bfloat16 [6, 4096, 128], P(None, 'col'), may hold values from -0.09375 to 0.09375
- low_ranks: int32 [6], replicated, may hold values from 1 to 4
- up_ranks: int32 [6], replicated, may hold values from 1 to 4
- inv_lower: bfloat16 [4, 4096, 4096], P(None, 'col', 'row'), may hold values from -0.09375 to 0.09375
- inv_upper: bfloat16 [4, 4096, 4096], P(None, 'col', 'row'), may hold values from -0.09375 to 0.09375
Outputs:
- solution: float32 [4, 1024, 4096], P(None, 'row', 'col')
Inputs may be any that keep to these rules, and one draw needn't show every extreme that they name: `low_ranks`: factor columns beyond 32 times this value are padding with arbitrary values and must be masked out. `up_ranks`: factor columns beyond 32 times this value are padding with arbitrary values and must be masked out.
All inputs are finite; a program needn't handle non-finite values.
Results may differ from a plain program's by a relative error of at most 0.03.
Values may be sent and summed in bfloat16 or wider, within the bound.
No kernel may reach another device: no remote copies, remote signals or barrier semaphores. Data moves between devices by JAX's collectives and lax.ppermute only.
A program may use at most 64 MiB of HBM per device.

v0:
```python
import jax
import jax.numpy as jnp
import numpy as np
from jax import lax
from jax.sharding import PartitionSpec as P

RBLK = 32


def laid_out(parts, dim):
    parts = jnp.moveaxis(parts, 0, dim)
    lengths = parts.shape
    return parts.reshape(*lengths[:dim], lengths[dim] * lengths[dim + 1], *lengths[dim + 2 :])


def from_everyone(value, axis):
    length = lax.axis_size(axis)
    return lax.all_to_all(
        jnp.broadcast_to(value[None], (length, *value.shape)), axis, 0, 0, tiled=True
    )


def gathered_copies(value, axis, dim):
    return laid_out(from_everyone(value, axis), dim)


def of_everyone(value, axis):
    everything = from_everyone(value, axis)
    return jnp.sum(everything.astype(jnp.float32), axis=0)


def rank_mask(ranks, pair_index, rank_cols):
    columns = jnp.arange(rank_cols, dtype=jnp.int32)
    return (columns[None, :] < RBLK * ranks[pair_index][:, None]).astype(jnp.float32)


def times_inverse(block, inverse):
    return lax.dot_general(
        block, inverse, (((1,), (1,)), ((), ())), preferred_element_type=jnp.float32
    )


def fold_columns(whole, piece):
    return times_inverse(whole, piece)


def shards(
    right_sides, low_left, low_right, up_left, up_right, low_ranks, up_ranks, inv_lower, inv_upper
):
    tile_count = right_sides.shape[0]
    rank_cols = low_left.shape[2]
    residual = right_sides
    forward = []
    for section in range(tile_count):
        rounded = residual[section].astype(jnp.bfloat16)
        whole = gathered_copies(rounded, "col", 1)
        solved = fold_columns(whole, lax.all_gather(inv_lower[section], "row", axis=1, tiled=True))
        forward.append(solved)
        if section + 1 < tile_count:
            pair_index = np.array(
                [tile * (tile - 1) // 2 + section for tile in range(section + 1, tile_count)],
                dtype=np.int32,
            )
            projections = jnp.einsum(
                "nw,mwr->mnr",
                solved.astype(jnp.bfloat16),
                low_right[pair_index],
                preferred_element_type=jnp.float32,
            )
            summed = of_everyone(projections.astype(jnp.bfloat16), "col").astype(jnp.float32)
            masked = (summed * rank_mask(low_ranks, pair_index, rank_cols)[:, None, :]).astype(
                jnp.bfloat16
            )
            update = jnp.einsum(
                "mnr,mwr->mnw", masked, low_left[pair_index], preferred_element_type=jnp.float32
            )
            residual = residual.at[section + 1 :].add(-update)
    state = jnp.stack(forward)
    solutions = [None] * tile_count
    for section in range(tile_count - 1, -1, -1):
        rounded = state[section].astype(jnp.bfloat16)
        whole = gathered_copies(rounded, "col", 1)
        solved = fold_columns(whole, lax.all_gather(inv_upper[section], "row", axis=1, tiled=True))
        solutions[section] = solved
        if section > 0:
            pair_index = np.array(
                [section * (section - 1) // 2 + tile for tile in range(section)], dtype=np.int32
            )
            projections = jnp.einsum(
                "nw,mwr->mnr",
                solved.astype(jnp.bfloat16),
                up_right[pair_index],
                preferred_element_type=jnp.float32,
            )
            summed = of_everyone(projections.astype(jnp.bfloat16), "col").astype(jnp.float32)
            masked = (summed * rank_mask(up_ranks, pair_index, rank_cols)[:, None, :]).astype(
                jnp.bfloat16
            )
            update = jnp.einsum(
                "mnr,mwr->mnw", masked, up_left[pair_index], preferred_element_type=jnp.float32
            )
            state = state.at[:section].add(-update)
    return jnp.stack(solutions)


def solution(mesh):
    in_specs = (
        P(None, "row", "col"),
        P(None, "col", None),
        P(None, "col", None),
        P(None, "col", None),
        P(None, "col", None),
        P(),
        P(),
        P(None, "col", "row"),
        P(None, "col", "row"),
    )
    out_specs = P(None, "row", "col")
    return jax.shard_map(shards, mesh=mesh, in_specs=in_specs, out_specs=out_specs, check_vma=False)
```

profile of v0, /device:TPU:1, one launch (start us, length us, event | category | flops | bytes accessed | tf_op | source)
XLA Modules:
  0.0 357.1 jit_solution(16431836217036689485)
XLA Ops:
  6.5 1.9 fusion.70
  8.6 0.7 all-gather.19.cloned.1.call-update
  9.3 0.7 all-gather.21.cloned.1.call-update
  10.6 1.9 fusion.69
  12.6 0.8 broadcast_in_dim.83
  13.4 7.6 %all-to-all-start = ((bf16[16,64,256]{2,1,0:T(8,128)(2,1)}), bf16[16,64,256]{2,1,0:T(8,128)(2,1)S(1)}, u32[]{:S(2)}, u32[]{:S(2)}) async-start(bf16[16,64,256]{2,1,0:T(8,128)(2,1)} %broadcast_in_dim.83), calls=%async_computation | async-start | bytes 1048576 | tf_op jit(solution)/shard_map/all_to_all | solution.py:18
  21.0 0.6 gather_fusion
  21.6 9.9 %all-to-all-done = bf16[16,64,256]{2,1,0:T(8,128)(2,1)S(1)} async-done(((bf16[16,64,256]{2,1,0:T(8,128)(2,1)}), bf16[16,64,256]{2,1,0:T(8,128)(2,1)S(1)}, u32[]{:S(2)}, u32[]{:S(2)}) %all-to-all-start) | async-done | bytes 524320 | tf_op jit(solution)/shard_map/all_to_all | solution.py:18
  31.6 22.7 %all-gather.17.cloned.1.call-done = bf16[1,256,4096]{2,1,0:T(8,128)(2,1)} async-done(((bf16[1,256,256]{2,1,0:T(8,128)(2,1)}), bf16[1,256,4096]{2,1,0:T(8,128)(2,1)}) %all-gather.17.cloned.1.call-update) | async-done | bytes 2097168 | tf_op jit(solution)/shard_map/all_gather | solution.py:57
  54.3 2.3 fusion.14
  56.8 1.1 broadcast_in_dim.85
  57.9 6.5 %all-to-all-start.1 = ((bf16[16,3,64,128]{3,2,1,0:T(8,128)(2,1)}), bf16[16,3,64,128]{3,2,1,0:T(8,128)(2,1)S(1)}, u32[]{:S(2)}, u32[]{:S(2)}) async-start(bf16[16,3,64,128]{3,2,1,0:T(8,128)(2,1)} %broadcast_in_dim.85), calls=%async_computation.1 | async-start | bytes 1572864 | tf_op jit(solution)/shard_map/all_to_all | solution.py:18
  65.7 0.6 gather_fusion.1
  66.4 11.7 %all-to-all-done.1 = bf16[16,3,64,128]{3,2,1,0:T(8,128)(2,1)S(1)} async-done(((bf16[16,3,64,128]{3,2,1,0:T(8,128)(2,1)}), bf16[16,3,64,128]{3,2,1,0:T(8,128)(2,1)S(1)}, u32[]{:S(2)}, u32[]{:S(2)}) %all-to-all-start.1) | async-done | bytes 786464 | tf_op jit(solution)/shard_map/all_to_all | solution.py:18
  78.4 0.8 broadcast_in_dim.89
  79.3 3.6 %all-to-all-start.2 = ((bf16[16,64,256]{2,1,0:T(8,128)(2,1)}), bf16[16,64,256]{2,1,0:T(8,128)(2,1)S(1)}, u32[]{:S(2)}, u32[]{:S(2)}) async-start(bf16[16,64,256]{2,1,0:T(8,128)(2,1)} %broadcast_in_dim.89), calls=%async_computation.2 | async-start | bytes 1048576 | tf_op jit(solution)/shard_map/all_to_all | solution.py:18
  83.5 9.5 %all-to-all-done.2 = bf16[16,64,256]{2,1,0:T(8,128)(2,1)S(1)} async-done(((bf16[16,64,256]{2,1,0:T(8,128)(2,1)}), bf16[16,64,256]{2,1,0:T(8,128)(2,1)S(1)}, u32[]{:S(2)}, u32[]{:S(2)}) %all-to-all-start.2) | async-done | bytes 524320 | tf_op jit(solution)/shard_map/all_to_all | solution.py:18
  93.1 3.1 all-gather.19.cloned.1.call-done
  96.2 2.4 fusion.12
  98.7 0.9 broadcast_in_dim.91
  99.7 6.5 %all-to-all-start.3 = ((bf16[16,2,64,128]{3,2,1,0:T(8,128)(2,1)}), bf16[16,2,64,128]{3,2,1,0:T(8,128)(2,1)S(1)}, u32[]{:S(2)}, u32[]{:S(2)}) async-start(bf16[16,2,64,128]{3,2,1,0:T(8,128)(2,1)} %broadcast_in_dim.91), calls=%async_computation.3 | async-start | bytes 1048576 | tf_op jit(solution)/shard_map/all_to_all | solution.py:18
  106.8 0.6 gather_fusion.4
  107.5 9.5 %all-to-all-done.3 = bf16[16,2,64,128]{3,2,1,0:T(8,128)(2,1)S(1)} async-done(((bf16[16,2,64,128]{3,2,1,0:T(8,128)(2,1)}), bf16[16,2,64,128]{3,2,1,0:T(8,128)(2,1)S(1)}, u32[]{:S(2)}, u32[]{:S(2)}) %all-to-all-start.3) | async-done | bytes 524320 | tf_op jit(solution)/shard_map/all_to_all | solution.py:18
  117.3 0.8 broadcast_in_dim.187
  118.1 3.6 %all-to-all-start.4 = ((bf16[16,64,256]{2,1,0:T(8,128)(2,1)}), bf16[16,64,256]{2,1,0:T(8,128)(2,1)S(1)}, u32[]{:S(2)}, u32[]{:S(2)}) async-start(bf16[16,64,256]{2,1,0:T(8,128)(2,1)} %broadcast_in_dim.187), calls=%async_computation.4 | async-start | bytes 1048576 | tf_op jit(solution)/shard_map/all_to_all | solution.py:18
  121.7 0.7 all-gather.29.cloned.1.call-update
  122.4 9.3 %all-to-all-done.4 = bf16[16,64,256]{2,1,0:T(8,128)(2,1)S(1)} async-done(((bf16[16,64,256]{2,1,0:T(8,128)(2,1)}), bf16[16,64,256]{2,1,0:T(8,128)(2,1)S(1)}, u32[]{:S(2)}, u32[]{:S(2)}) %all-to-all-start.4) | async-done | bytes 524320 | tf_op jit(solution)/shard_map/all_to_all | solution.py:18
  131.8 6.3 %all-gather.21.cloned.1.call-done = bf16[1,256,4096]{2,1,0:T(8,128)(2,1)} async-done(((bf16[1,256,256]{2,1,0:T(8,128)(2,1)}), bf16[1,256,4096]{2,1,0:T(8,128)(2,1)}) %all-gather.21.cloned.1.call-update) | async-done | bytes 2097168 | tf_op jit(solution)/shard_map/all_gather | solution.py:57
  138.1 2.4 fusion.10
  140.6 0.8 broadcast_in_dim.191
  141.3 6.5 %all-to-all-start.5 = ((bf16[16,1,64,128]{3,2,1,0:T(8,128)(2,1)}), bf16[16,1,64,128]{3,2,1,0:T(8,128)(2,1)S(1)}, u32[]{:S(2)}, u32[]{:S(2)}) async-start(bf16[16,1,64,128]{3,2,1,0:T(8,128)(2,1)} %broadcast_in_dim.191), calls=%async_computation.5 | async-start | bytes 524288 | tf_op jit(solution)/shard_map/all_to_all | solution.py:18
  149.0 7.1 %all-to-all-done.5 = bf16[16,1,64,128]{3,2,1,0:T(8,128)(2,1)S(1)} async-done(((bf16[16,1,64,128]{3,2,1,0:T(8,128)(2,1)}), bf16[16,1,64,128]{3,2,1,0:T(8,128)(2,1)S(1)}, u32[]{:S(2)}, u32[]{:S(2)}) %all-to-all-start.5) | async-done | bytes 262176 | tf_op jit(solution)/shard_map/all_to_all | solution.py:18
  156.3 12.8 %all_to_all.70 = bf16[16,64,256]{2,1,0:T(8,128)(2,1)S(1)} all-to-all(bf16[16,64,256]{2,1,0:T(8,128)(2,1)S(1)} %broadcast_in_dim.195), channel_id=1, replica_groups=mesh['row'=16,'col'=16] {'col'}, dimensions={0} | all-to-all | bytes 1048576 | tf_op jit(solution)/shard_map/all_to_all | solution.py:18
  169.2 10.6 %all-gather.23.cloned.1.call-done = bf16[1,256,4096]{2,1,0:T(8,128)(2,1)} async-done(((bf16[1,256,256]{2,1,0:T(8,128)(2,1)}), bf16[1,256,4096]{2,1,0:T(8,128)(2,1)}) %all-gather.23.cloned.1.call-update) | async-done | bytes 2097168 | tf_op jit(solution)/shard_map/all_gather | solution.py:57
  179.8 2.4 fusion.31
  182.2 0.8 broadcast_in_dim.196
  183.1 6.5 %all-to-all-start.7 = ((bf16[16,64,256]{2,1,0:T(8,128)(2,1)}), bf16[16,64,256]{2,1,0:T(8,128)(2,1)S(1)}, u32[]{:S(2)}, u32[]{:S(2)}) async-start(bf16[16,64,256]{2,1,0:T(8,128)(2,1)} %broadcast_in_dim.196), calls=%async_computation.7 | async-start | bytes 1048576 | tf_op jit(solution)/shard_map/all_to_all | solution.py:18
  190.2 10.2 %all-to-all-done.7 = bf16[16,64,256]{2,1,0:T(8,128)(2,1)S(1)} async-done(((bf16[16,64,256]{2,1,0:T(8,128)(2,1)}), bf16[16,64,256]{2,1,0:T(8,128)(2,1)S(1)}, u32[]{:S(2)}, u32[]{:S(2)}) %all-to-all-start.7) | async-done | bytes 524320 | tf_op jit(solution)/shard_map/all_to_all | solution.py:18
  200.5 21.2 %all-gather.25.cloned.1.call-done = bf16[1,256,4096]{2,1,0:T(8,128)(2,1)} async-done(((bf16[1,256,256]{2,1,0:T(8,128)(2,1)}), bf16[1,256,4096]{2,1,0:T(8,128)(2,1)}) %all-gather.25.cloned.1.call-update) | async-done | bytes 2097168 | tf_op jit(solution)/shard_map/all_gather | solution.py:83
  221.6 2.4 fusion.6
  224.2 1.1 broadcast_in_dim.197
  225.3 6.5 %all-to-all-start.8 = ((bf16[16,3,64,128]{3,2,1,0:T(8,128)(2,1)}), bf16[16,3,64,128]{3,2,1,0:T(8,128)(2,1)S(1)}, u32[]{:S(2)}, u32[]{:S(2)}) async-start(bf16[16,3,64,128]{3,2,1,0:T(8,128)(2,1)} %broadcast_in_dim.197), calls=%async_computation.8 | async-start | bytes 1572864 | tf_op jit(solution)/shard_map/all_to_all | solution.py:18
  232.4 0.6 gather_fusion.7
  233.2 12.3 %all-to-all-done.8 = bf16[16,3,64,128]{3,2,1,0:T(8,128)(2,1)S(1)} async-done(((bf16[16,3,64,128]{3,2,1,0:T(8,128)(2,1)}), bf16[16,3,64,128]{3,2,1,0:T(8,128)(2,1)S(1)}, u32[]{:S(2)}, u32[]{:S(2)}) %all-to-all-start.8) | async-done | bytes 786464 | tf_op jit(solution)/shard_map/all_to_all | solution.py:18
  245.8 0.8 broadcast_in_dim.202
  246.6 3.6 %all-to-all-start.9 = ((bf16[16,64,256]{2,1,0:T(8,128)(2,1)}), bf16[16,64,256]{2,1,0:T(8,128)(2,1)S(1)}, u32[]{:S(2)}, u32[]{:S(2)}) async-start(bf16[16,64,256]{2,1,0:T(8,128)(2,1)} %broadcast_in_dim.202), calls=%async_computation.9 | async-start | bytes 1048576 | tf_op jit(solution)/shard_map/all_to_all | solution.py:18
  250.3 0.7 all-gather.31.cloned.1.call-update
  251.6 8.8 %all-to-all-done.9 = bf16[16,64,256]{2,1,0:T(8,128)(2,1)S(1)} async-done(((bf16[16,64,256]{2,1,0:T(8,128)(2,1)}), bf16[16,64,256]{2,1,0:T(8,128)(2,1)S(1)}, u32[]{:S(2)}, u32[]{:S(2)}) %all-to-all-start.9) | async-done | bytes 524320 | tf_op jit(solution)/shard_map/all_to_all | solution.py:18
  260.5 2.9 all-gather.27.cloned.1.call-done
  263.4 2.3 fusion.4
  265.9 0.9 broadcast_in_dim.203
  266.8 6.5 %all-to-all-start.10 = ((bf16[16,2,64,128]{3,2,1,0:T(8,128)(2,1)}), bf16[16,2,64,128]{3,2,1,0:T(8,128)(2,1)S(1)}, u32[]{:S(2)}, u32[]{:S(2)}) async-start(bf16[16,2,64,128]{3,2,1,0:T(8,128)(2,1)} %broadcast_in_dim.203), calls=%async_computation.10 | async-start | bytes 1048576 | tf_op jit(solution)/shard_map/all_to_all | solution.py:18
  273.9 0.6 gather_fusion.10
  274.7 9.5 %all-to-all-done.10 = bf16[16,2,64,128]{3,2,1,0:T(8,128)(2,1)S(1)} async-done(((bf16[16,2,64,128]{3,2,1,0:T(8,128)(2,1)}), bf16[16,2,64,128]{3,2,1,0:T(8,128)(2,1)S(1)}, u32[]{:S(2)}, u32[]{:S(2)}) %all-to-all-start.10) | async-done | bytes 524320 | tf_op jit(solution)/shard_map/all_to_all | solution.py:18
  284.5 13.4 %all_to_all.71 = bf16[16,64,256]{2,1,0:T(8,128)(2,1)S(1)} all-to-all(bf16[16,64,256]{2,1,0:T(8,128)(2,1)S(1)} %broadcast_in_dim.208), channel_id=1, replica_groups=mesh['row'=16,'col'=16] {'col'}, dimensions={0} | all-to-all | bytes 1048576 | tf_op jit(solution)/shard_map/all_to_all | solution.py:18
  297.9 7.4 %all-gather.29.cloned.1.call-done = bf16[1,256,4096]{2,1,0:T(8,128)(2,1)} async-done(((bf16[1,256,256]{2,1,0:T(8,128)(2,1)}), bf16[1,256,4096]{2,1,0:T(8,128)(2,1)}) %all-gather.29.cloned.1.call-update) | async-done | bytes 2097168 | tf_op jit(solution)/shard_map/all_gather | solution.py:83
  305.3 2.4 fusion.2
  307.7 0.8 broadcast_in_dim.210
  308.5 6.5 %all-to-all-start.12 = ((bf16[16,1,64,128]{3,2,1,0:T(8,128)(2,1)}), bf16[16,1,64,128]{3,2,1,0:T(8,128)(2,1)S(1)}, u32[]{:S(2)}, u32[]{:S(2)}) async-start(bf16[16,1,64,128]{3,2,1,0:T(8,128)(2,1)} %broadcast_in_dim.210), calls=%async_computation.12 | async-start | bytes 524288 | tf_op jit(solution)/shard_map/all_to_all | solution.py:18
  315.1 8.2 %all-to-all-done.12 = bf16[16,1,64,128]{3,2,1,0:T(8,128)(2,1)S(1)} async-done(((bf16[16,1,64,128]{3,2,1,0:T(8,128)(2,1)}), bf16[16,1,64,128]{3,2,1,0:T(8,128)(2,1)S(1)}, u32[]{:S(2)}, u32[]{:S(2)}) %all-to-all-start.12) | async-done | bytes 262176 | tf_op jit(solution)/shard_map/all_to_all | solution.py:18
  323.5 12.8 %all_to_all.72 = bf16[16,64,256]{2,1,0:T(8,128)(2,1)S(1)} all-to-all(bf16[16,64,256]{2,1,0:T(8,128)(2,1)S(1)} %broadcast_in_dim.214), channel_id=1, replica_groups=mesh['row'=16,'col'=16] {'col'}, dimensions={0} | all-to-all | bytes 1048576 | tf_op jit(solution)/shard_map/all_to_all | solution.py:18
  336.4 10.8 %all-gather.31.cloned.1.call-done = bf16[1,256,4096]{2,1,0:T(8,128)(2,1)} async-done(((bf16[1,256,256]{2,1,0:T(8,128)(2,1)}), bf16[1,256,4096]{2,1,0:T(8,128)(2,1)}) %all-gather.31.cloned.1.call-update) | async-done | bytes 2097168 | tf_op jit(solution)/shard_map/all_gather | solution.py:83
  347.1 2.3 fusion.24
  349.5 0.7 pad_maximum_fusion
  (90 shorter events, 9.2 us)
Async XLA Ops:
  6.5 14.5 %copy-start.10 = (s32[3]{0:T(128)S(1)}, s32[3]{0:T(128)}, u32[]{:S(2)}) copy-start(s32[3]{0:T(128)} %constant.313) | copy-start | bytes 40
  6.5 6.0 %copy-start.6 = (f32[4,64,256]{2,1,0:T(8,128)S(1)}, f32[4,64,256]{2,1,0:T(8,128)}, u32[]{:S(2)}) copy-start(f32[4,64,256]{2,1,0:T(8,128)} %param.45) | copy-start | bytes 786436
  6.5 14.5 %copy-start.2 = (bf16[6,256,128]{2,1,0:T(8,128)(2,1)S(1)}, bf16[6,256,128]{2,1,0:T(8,128)(2,1)}, u32[]{:S(2)}) copy-start(bf16[6,256,128]{2,1,0:T(8,128)(2,1)} %param.47) | copy-start | bytes 1179652
  6.5 47.7 %all-gather.17.cloned.1.call-start = ((), (), s32[]{:S(2)}) async-start(), calls=%async_computation.14 | async-start | bytes 2228224 | tf_op jit(solution)/shard_map/all_gather | solution.py:57
  8.5 87.7 %all-gather.19.cloned.1.call-start = ((), (), s32[]{:S(2)}) async-start(), calls=%async_computation.15 | async-start | bytes 2228224 | tf_op jit(solution)/shard_map/all_gather | solution.py:57
  9.3 128.8 %all-gather.21.cloned.1.call-start = ((), (), s32[]{:S(2)}) async-start(), calls=%async_computation.16 | async-start | bytes 2228224 | tf_op jit(solution)/shard_map/all_gather | solution.py:57
  10.0 169.8 %all-gather.23.cloned.1.call-start = ((), (), s32[]{:S(2)}) async-start(), calls=%async_computation.17 | async-start | bytes 2228224 | tf_op jit(solution)/shard_map/all_gather | solution.py:57
  10.6 211.0 %all-gather.25.cloned.1.call-start = ((), (), s32[]{:S(2)}) async-start(), calls=%async_computation.18 | async-start | bytes 2228224 | tf_op jit(solution)/shard_map/all_gather | solution.py:83
  13.4 18.1 %all-to-all-start = ((bf16[16,64,256]{2,1,0:T(8,128)(2,1)}), bf16[16,64,256]{2,1,0:T(8,128)(2,1)S(1)}, u32[]{:S(2)}, u32[]{:S(2)}) async-start(bf16[16,64,256]{2,1,0:T(8,128)(2,1)} %broadcast_in_dim.83), calls=%async_computation | async-start | bytes 1048576 | tf_op jit(solution)/shard_map/all_to_all | solution.py:18
  56.6 8.4 %copy-start.3 = (bf16[6,256,128]{2,1,0:T(8,128)(2,1)S(1)}, bf16[6,256,128]{2,1,0:T(8,128)(2,1)}, u32[]{:S(2)}) copy-start(bf16[6,256,128]{2,1,0:T(8,128)(2,1)} %param.46) | copy-start | bytes 1179652
  56.6 9.0 %copy-start = (s32[6]{0:T(128)S(1)}, s32[6]{0:T(128)}, u32[]{:S(2)}) copy-start(s32[6]{0:T(128)} %param.50) | copy-start | bytes 76
  57.9 20.2 %all-to-all-start.1 = ((bf16[16,3,64,128]{3,2,1,0:T(8,128)(2,1)}), bf16[16,3,64,128]{3,2,1,0:T(8,128)(2,1)S(1)}, u32[]{:S(2)}, u32[]{:S(2)}) async-start(bf16[16,3,64,128]{3,2,1,0:T(8,128)(2,1)} %broadcast_in_dim.85), calls=%async_computation.1 | async-start | bytes 1572864 | tf_op jit(solution)/shard_map/all_to_all | solution.py:18
  64.4 198.9 %all-gather.27.cloned.1.call-start = ((), (), s32[]{:S(2)}) async-start(), calls=%async_computation.19 | async-start | bytes 2228224 | tf_op jit(solution)/shard_map/all_gather | solution.py:83
  65.0 17.9 %copy-start.9 = (s32[2]{0:T(128)S(1)}, s32[2]{0:T(128)}, u32[]{:S(2)}) copy-start(s32[2]{0:T(128)} %constant.316) | copy-start | bytes 28
  79.3 13.8 %all-to-all-start.2 = ((bf16[16,64,256]{2,1,0:T(8,128)(2,1)}), bf16[16,64,256]{2,1,0:T(8,128)(2,1)S(1)}, u32[]{:S(2)}, u32[]{:S(2)}) async-start(bf16[16,64,256]{2,1,0:T(8,128)(2,1)} %broadcast_in_dim.89), calls=%async_computation.2 | async-start | bytes 1048576 | tf_op jit(solution)/shard_map/all_to_all | solution.py:18
  99.7 17.4 %all-to-all-start.3 = ((bf16[16,2,64,128]{3,2,1,0:T(8,128)(2,1)}), bf16[16,2,64,128]{3,2,1,0:T(8,128)(2,1)S(1)}, u32[]{:S(2)}, u32[]{:S(2)}) async-start(bf16[16,2,64,128]{3,2,1,0:T(8,128)(2,1)} %broadcast_in_dim.91), calls=%async_computation.3 | async-start | bytes 1048576 | tf_op jit(solution)/shard_map/all_to_all | solution.py:18
  118.1 13.6 %all-to-all-start.4 = ((bf16[16,64,256]{2,1,0:T(8,128)(2,1)}), bf16[16,64,256]{2,1,0:T(8,128)(2,1)S(1)}, u32[]{:S(2)}, u32[]{:S(2)}) async-start(bf16[16,64,256]{2,1,0:T(8,128)(2,1)} %broadcast_in_dim.187), calls=%async_computation.4 | async-start | bytes 1048576 | tf_op jit(solution)/shard_map/all_to_all | solution.py:18
  121.7 183.6 %all-gather.29.cloned.1.call-start = ((), (), s32[]{:S(2)}) async-start(), calls=%async_computation.20 | async-start | bytes 2228224 | tf_op jit(solution)/shard_map/all_gather | solution.py:83
  141.3 14.8 %all-to-all-start.5 = ((bf16[16,1,64,128]{3,2,1,0:T(8,128)(2,1)}), bf16[16,1,64,128]{3,2,1,0:T(8,128)(2,1)S(1)}, u32[]{:S(2)}, u32[]{:S(2)}) async-start(bf16[16,1,64,128]{3,2,1,0:T(8,128)(2,1)} %broadcast_in_dim.191), calls=%async_computation.5 | async-start | bytes 524288 | tf_op jit(solution)/shard_map/all_to_all | solution.py:18
  179.8 9.8 %copy-start.8 = (s32[3]{0:T(128)S(1)}, s32[3]{0:T(128)}, u32[]{:S(2)}) copy-start(s32[3]{0:T(128)} %constant.319) | copy-start | bytes 40
  179.8 9.8 %copy-start.4 = (bf16[6,256,128]{2,1,0:T(8,128)(2,1)S(1)}, bf16[6,256,128]{2,1,0:T(8,128)(2,1)}, u32[]{:S(2)}) copy-start(bf16[6,256,128]{2,1,0:T(8,128)(2,1)} %param.49) | copy-start | bytes 1179652
  183.1 17.4 %all-to-all-start.7 = ((bf16[16,64,256]{2,1,0:T(8,128)(2,1)}), bf16[16,64,256]{2,1,0:T(8,128)(2,1)S(1)}, u32[]{:S(2)}, u32[]{:S(2)}) async-start(bf16[16,64,256]{2,1,0:T(8,128)(2,1)} %broadcast_in_dim.196), calls=%async_computation.7 | async-start | bytes 1048576 | tf_op jit(solution)/shard_map/all_to_all | solution.py:18
  221.6 10.2 %copy-start.5 = (bf16[6,256,128]{2,1,0:T(8,128)(2,1)S(1)}, bf16[6,256,128]{2,1,0:T(8,128)(2,1)}, u32[]{:S(2)}) copy-start(bf16[6,256,128]{2,1,0:T(8,128)(2,1)} %param.48) | copy-start | bytes 1179652
  224.0 8.4 %copy-start.1 = (s32[6]{0:T(128)S(1)}, s32[6]{0:T(128)}, u32[]{:S(2)}) copy-start(s32[6]{0:T(128)} %param.51) | copy-start | bytes 76
  225.3 20.2 %all-to-all-start.8 = ((bf16[16,3,64,128]{3,2,1,0:T(8,128)(2,1)}), bf16[16,3,64,128]{3,2,1,0:T(8,128)(2,1)S(1)}, u32[]{:S(2)}, u32[]{:S(2)}) async-start(bf16[16,3,64,128]{3,2,1,0:T(8,128)(2,1)} %broadcast_in_dim.197), calls=%async_computation.8 | async-start | bytes 1572864 | tf_op jit(solution)/shard_map/all_to_all | solution.py:18
  231.8 19.2 %copy-start.7 = (s32[2]{0:T(128)S(1)}, s32[2]{0:T(128)}, u32[]{:S(2)}) copy-start(s32[2]{0:T(128)} %constant.322) | copy-start | bytes 28
  246.6 13.8 %all-to-all-start.9 = ((bf16[16,64,256]{2,1,0:T(8,128)(2,1)}), bf16[16,64,256]{2,1,0:T(8,128)(2,1)S(1)}, u32[]{:S(2)}, u32[]{:S(2)}) async-start(bf16[16,64,256]{2,1,0:T(8,128)(2,1)} %broadcast_in_dim.202), calls=%async_computation.9 | async-start | bytes 1048576 | tf_op jit(solution)/shard_map/all_to_all | solution.py:18
  250.3 96.9 %all-gather.31.cloned.1.call-start = ((), (), s32[]{:S(2)}) async-start(), calls=%async_computation.21 | async-start | bytes 2228224 | tf_op jit(solution)/shard_map/all_gather | solution.py:83
  266.8 17.4 %all-to-all-start.10 = ((bf16[16,2,64,128]{3,2,1,0:T(8,128)(2,1)}), bf16[16,2,64,128]{3,2,1,0:T(8,128)(2,1)S(1)}, u32[]{:S(2)}, u32[]{:S(2)}) async-start(bf16[16,2,64,128]{3,2,1,0:T(8,128)(2,1)} %broadcast_in_dim.203), calls=%async_computation.10 | async-start | bytes 1048576 | tf_op jit(solution)/shard_map/all_to_all | solution.py:18
  308.5 14.7 %all-to-all-start.12 = ((bf16[16,1,64,128]{3,2,1,0:T(8,128)(2,1)}), bf16[16,1,64,128]{3,2,1,0:T(8,128)(2,1)S(1)}, u32[]{:S(2)}, u32[]{:S(2)}) async-start(bf16[16,1,64,128]{3,2,1,0:T(8,128)(2,1)} %broadcast_in_dim.210), calls=%async_computation.12 | async-start | bytes 524288 | tf_op jit(solution)/shard_map/all_to_all | solution.py:18
Sparse Core Ops, SparseCore 0:
  9.1 45.1 all-gather.16
  56.0 40.1 all-gather.18
  98.0 40.0 all-gather.20
  139.7 40.0 all-gather.22
  181.4 40.1 all-gather.24
  223.2 40.1 all-gather.26
  265.1 40.0 all-gather.28
  307.0 40.0 all-gather.30
where the time goes:
time: 359 us; the launch traced here: 357 us
  waiting for transfers between devices  195 us (54%)
  starting transfers between devices  64.4 us (18%)
  blocking collectives  39 us (11%)
  local copies, waits for them, and re-layouts  21.9 us (6%)
  matrix products  20.8 us (6%)
  between operations  14.5 us (4%)
    all_to_all x11, waiting for transfers between devices, from_everyone(): lax.all_to_all(jnp.broadcast_to(value[None], (length, *value.shape)), axi...  106 us
    all_to_all x11, starting transfers between devices, from_everyone(): lax.all_to_all(jnp.broadcast_to(value[None], (length, *value.shape)), axi...  64.1 us
    all_gather x4, waiting for transfers between devices, shards(): lax.all_gather(inv_lower[section], 'row', axis=1, tiled=True)  42.8 us
    all_gather x4, waiting for transfers between devices, shards(): lax.all_gather(inv_upper[section], 'row', axis=1, tiled=True)  42.2 us
    all_to_all x3, blocking collectives, from_everyone(): lax.all_to_all(jnp.broadcast_to(value[None], (length, *value.shape)), axi...  39 us
    dot_general x8, matrix products, times_inverse(): lax.dot_general(block, inverse, (((1,), (1,)), ((), ())), preferred_eleme...  18.9 us
    broadcast_in_dim x19, local copies, waits for them, and re-layouts, from_everyone(): jnp.broadcast_to(value[None], (length, *value.shape))  9.98 us
  transfers between devices with their start and end apart: 19, of which 19 were waited for; matrix products, arithmetic and copies ran while one was open for 11% of the time, Pallas kernels for 0%

commit v1 on v0

--- a/solution.py
+++ b/solution.py
@@ -5,6 +5,19 @@
 from jax.sharding import PartitionSpec as P
 
 RBLK = 32
+
+
+def ring_gather(array, axis, dim):
+    ways = lax.axis_size(axis)
+    up = [(d, (d + 1) % ways) for d in range(ways)]
+    down = [(d, (d - 1) % ways) for d in range(ways)]
+    earlier, later = ([array], [array])
+    for _ in range(ways // 2):
+        earlier.append(lax.ppermute(earlier[-1], axis, up))
+    for _ in range((ways - 1) // 2):
+        later.append(lax.ppermute(later[-1], axis, down))
+    line = jnp.concatenate([*earlier[::-1], *later[1:]], axis=dim)
+    return jnp.roll(line, (lax.axis_index(axis) - ways // 2) * array.shape[dim], axis=dim)
 
 
 def laid_out(parts, dim):
@@ -80,7 +93,7 @@
     for section in range(tile_count - 1, -1, -1):
         rounded = state[section].astype(jnp.bfloat16)
         whole = gathered_copies(rounded, "col", 1)
-        solved = fold_columns(whole, lax.all_gather(inv_upper[section], "row", axis=1, tiled=True))
+        solved = fold_columns(whole, ring_gather(inv_upper[section], "row", 1))
         solutions[section] = solved
         if section > 0:
             pair_index = np.array(

time: 359 us -> 343 us (0.955)
  waiting for transfers between devices: 195 us -> 46.5 us
  starting transfers between devices: 64.4 us -> 155 us
  local copies, waits for them, and re-layouts: 21.9 us -> 97.5 us
  blocking collectives: 39 us -> 0 us
    ppermute x0 -> x60, starting transfers between devices: none -> 83.2 us  [the longest x28 52.3 us: ring_gather(): later.append(lax.ppermute(later[-1], axis, down))]
    unnamed x22 -> x153, local copies, waits for them, and re-layouts: 0.05 us -> 67.4 us
    all_to_all x11 -> x14, waiting for transfers between devices: 106 us -> 39.1 us  [from_everyone(): lax.all_to_all(jnp.broadcast_to(value[None], (length, *value.shape)), axi...]
    all_gather x4, waiting for transfers between devices: 42.8 us -> 0.06 us  [shards(): lax.all_gather(inv_lower[section], 'row', axis=1, tiled=True)]
    all_gather x4 -> x0, waiting for transfers between devices: 42.2 us -> none  [shards(): lax.all_gather(inv_upper[section], 'row', axis=1, tiled=True)]
    all_to_all x3 -> x0, blocking collectives: 39 us -> none  [from_everyone(): lax.all_to_all(jnp.broadcast_to(value[None], (length, *value.shape)), axi...]
    all_to_all x11 -> x14, starting transfers between devices: 64.1 us -> 71.7 us  [from_everyone(): lax.all_to_all(jnp.broadcast_to(value[None], (length, *value.shape)), axi...]
    ppermute x0 -> x60, waiting for transfers between devices: none -> 5.47 us  [the longest x28 5 us: ring_gather(): later.append(lax.ppermute(later[-1], axis, down))]
  transfers between devices with their start and end apart: 19 -> 78, of which waited for: 19 -> 13; matrix products, arithmetic and copies ran while one was open for 11% -> 35% of each run, Pallas kernels for 0% -> 0%
where the time goes in v1:
time: 343 us; the launch traced here: 339 us
  starting transfers between devices  155 us (45%)
  local copies, waits for them, and re-layouts  97.5 us (28%)
  waiting for transfers between devices  46.5 us (14%)
  matrix products  21.4 us (6%)
  between operations  14.8 us (4%)
    all_to_all x14, starting transfers between devices, from_everyone(): lax.all_to_all(jnp.broadcast_to(value[None], (length, *value.shape)), axi...  71.7 us
    unnamed x153, local copies, waits for them, and re-layouts  67.4 us
    ppermute x28, starting transfers between devices, ring_gather(): later.append(lax.ppermute(later[-1], axis, down))  52.3 us
    all_to_all x14, waiting for transfers between devices, from_everyone(): lax.all_to_all(jnp.broadcast_to(value[None], (length, *value.shape)), axi...  39.1 us
    ppermute x32, starting transfers between devices, ring_gather(): earlier.append(lax.ppermute(earlier[-1], axis, up))  31 us
    dot_general x8, matrix products, times_inverse(): lax.dot_general(block, inverse, (((1,), (1,)), ((), ())), preferred_eleme...  19.6 us
    broadcast_in_dim x19, local copies, waits for them, and re-layouts, from_everyone(): jnp.broadcast_to(value[None], (length, *value.shape))  12.6 us
  transfers between devices with their start and end apart: 78, of which 13 were waited for; matrix products, arithmetic and copies ran while one was open for 35% of the time, Pallas kernels for 0%

profile of v1, /device:TPU:1, one launch (start us, length us, event | category | flops | bytes accessed | tf_op | source)
XLA Modules:
  0.0 338.7 jit_solution(14593260002806433008)
XLA Ops:
  6.5 1.9 fusion.81
  10.0 1.8 slice_bitcast_fusion
  11.9 3.0 collective-permute-start.15
  17.4 2.1 collective-permute-start.16
  20.4 6.9 %all-to-all-start = ((bf16[16,64,256]{2,1,0:T(8,128)(2,1)}), bf16[16,64,256]{2,1,0:T(8,128)(2,1)S(1)}, u32[]{:S(2)}, u32[]{:S(2)}) async-start(bf16[16,64,256]{2,1,0:T(8,128)(2,1)} %broadcast_in_dim.83), calls=%async_computation | async-start | bytes 1048576 | tf_op jit(solution)/shard_map/all_to_all | solution.py:31
  28.2 2.4 collective-permute-start.17
  32.7 2.2 collective-permute-start.32
  35.5 3.1 collective-permute-start.23
  38.8 1.7 collective-permute-start.33
  42.1 2.3 collective-permute-start.9
  44.4 1.8 collective-permute-start.48
  46.6 2.4 collective-permute-start.34
  50.5 4.5 %collective-permute-start.10 = (bf16[256,256]{1,0:T(8,128)(2,1)S(1)}, bf16[256,256]{1,0:T(8,128)(2,1)}, u32[]{:S(2)}, u32[]{:S(2)}) collective-permute-start(bf16[256,256]{1,0:T(8,128)(2,1)S(1)} %collective-permute-done.9), channel_id=1, source_target_pairs={{0,240},{16,0},{32,16},{48,32},{64,48},{80,64},{96,80},{112,96},{1... | collective-permute-start | bytes 393224 | tf_op jit(solution)/shard_map/ppermute | solution.py:18
  56.4 1.8 collective-permute-start.21
  58.8 2.4 collective-permute-start.11
  61.3 2.0 collective-permute-start.36
  71.3 4.1 %collective-permute-start.24 = (bf16[256,256]{1,0:T(8,128)(2,1)S(1)}, bf16[256,256]{1,0:T(8,128)(2,1)}, u32[]{:S(2)}, u32[]{:S(2)}) collective-permute-start(bf16[256,256]{1,0:T(8,128)(2,1)S(1)} %collective-permute-done.23), channel_id=1, source_target_pairs={{0,240},{16,0},{32,16},{48,32},{64,48},{80,64},{96,80},{112,96},{1... | collective-permute-start | bytes 393224 | tf_op jit(solution)/shard_map/ppermute | solution.py:18
  75.4 3.0 collective-permute-start.12
  81.6 1.6 constant_dynamic-update-slice_fusion.29
  86.2 2.3 fusion.10
  89.9 6.9 %all-to-all-start.1 = ((bf16[16,3,64,128]{3,2,1,0:T(8,128)(2,1)}), bf16[16,3,64,128]{3,2,1,0:T(8,128)(2,1)S(1)}, u32[]{:S(2)}, u32[]{:S(2)}) async-start(bf16[16,3,64,128]{3,2,1,0:T(8,128)(2,1)} %broadcast_in_dim.85), calls=%async_computation.1 | async-start | bytes 1572864 | tf_op jit(solution)/shard_map/all_to_all | solution.py:31
  98.9 2.7 collective-permute-start.25
  108.1 1.6 constant_dynamic-update-slice_fusion.44
  111.6 6.7 %all-to-all-start.2 = ((bf16[16,64,256]{2,1,0:T(8,128)(2,1)}), bf16[16,64,256]{2,1,0:T(8,128)(2,1)S(1)}, u32[]{:S(2)}, u32[]{:S(2)}) async-start(bf16[16,64,256]{2,1,0:T(8,128)(2,1)} %broadcast_in_dim.89), calls=%async_computation.2 | async-start | bytes 1048576 | tf_op jit(solution)/shard_map/all_to_all | solution.py:31
  122.9 2.2 collective-permute-start.39
  125.9 1.7 collective-permute-start.7
  130.8 2.4 fusion.8
  134.3 6.9 %all-to-all-start.3 = ((bf16[16,2,64,128]{3,2,1,0:T(8,128)(2,1)}), bf16[16,2,64,128]{3,2,1,0:T(8,128)(2,1)S(1)}, u32[]{:S(2)}, u32[]{:S(2)}) async-start(bf16[16,2,64,128]{3,2,1,0:T(8,128)(2,1)} %broadcast_in_dim.91), calls=%async_computation.3 | async-start | bytes 1048576 | tf_op jit(solution)/shard_map/all_to_all | solution.py:31
  146.6 6.0 %all-to-all-done.3 = bf16[16,2,64,128]{3,2,1,0:T(8,128)(2,1)S(1)} async-done(((bf16[16,2,64,128]{3,2,1,0:T(8,128)(2,1)}), bf16[16,2,64,128]{3,2,1,0:T(8,128)(2,1)S(1)}, u32[]{:S(2)}, u32[]{:S(2)}) %all-to-all-start.3) | async-done | bytes 524320 | tf_op jit(solution)/shard_map/all_to_all | solution.py:31
  153.7 3.6 %all-to-all-start.4 = ((bf16[16,64,256]{2,1,0:T(8,128)(2,1)}), bf16[16,64,256]{2,1,0:T(8,128)(2,1)S(1)}, u32[]{:S(2)}, u32[]{:S(2)}) async-start(bf16[16,64,256]{2,1,0:T(8,128)(2,1)} %broadcast_in_dim.187), calls=%async_computation.4 | async-start | bytes 1048576 | tf_op jit(solution)/shard_map/all_to_all | solution.py:31
  162.7 1.6 constant_dynamic-update-slice_fusion.12
  164.4 3.9 %all-to-all-done.4 = bf16[16,64,256]{2,1,0:T(8,128)(2,1)S(1)} async-done(((bf16[16,64,256]{2,1,0:T(8,128)(2,1)}), bf16[16,64,256]{2,1,0:T(8,128)(2,1)S(1)}, u32[]{:S(2)}, u32[]{:S(2)}) %all-to-all-start.4) | async-done | bytes 524320 | tf_op jit(solution)/shard_map/all_to_all | solution.py:31
  168.4 2.4 fusion.6
  171.7 3.5 %all-to-all-start.5 = ((bf16[16,1,64,128]{3,2,1,0:T(8,128)(2,1)}), bf16[16,1,64,128]{3,2,1,0:T(8,128)(2,1)S(1)}, u32[]{:S(2)}, u32[]{:S(2)}) async-start(bf16[16,1,64,128]{3,2,1,0:T(8,128)(2,1)} %broadcast_in_dim.191), calls=%async_computation.5 | async-start | bytes 524288 | tf_op jit(solution)/shard_map/all_to_all | solution.py:31
  175.3 1.6 constant_dynamic-update-slice_fusion.11
  179.2 3.6 %all-to-all-done.5 = bf16[16,1,64,128]{3,2,1,0:T(8,128)(2,1)S(1)} async-done(((bf16[16,1,64,128]{3,2,1,0:T(8,128)(2,1)}), bf16[16,1,64,128]{3,2,1,0:T(8,128)(2,1)S(1)}, u32[]{:S(2)}, u32[]{:S(2)}) %all-to-all-start.5) | async-done | bytes 262176 | tf_op jit(solution)/shard_map/all_to_all | solution.py:31
  183.9 3.6 %all-to-all-start.6 = ((bf16[16,64,256]{2,1,0:T(8,128)(2,1)}), bf16[16,64,256]{2,1,0:T(8,128)(2,1)S(1)}, u32[]{:S(2)}, u32[]{:S(2)}) async-start(bf16[16,64,256]{2,1,0:T(8,128)(2,1)} %broadcast_in_dim.195), calls=%async_computation.6 | async-start | bytes 1048576 | tf_op jit(solution)/shard_map/all_to_all | solution.py:31
  190.4 6.4 %all-to-all-done.6 = bf16[16,64,256]{2,1,0:T(8,128)(2,1)S(1)} async-done(((bf16[16,64,256]{2,1,0:T(8,128)(2,1)}), bf16[16,64,256]{2,1,0:T(8,128)(2,1)S(1)}, u32[]{:S(2)}, u32[]{:S(2)}) %all-to-all-start.6) | async-done | bytes 524320 | tf_op jit(solution)/shard_map/all_to_all | solution.py:31
  196.8 2.4 fusion.35
  200.1 3.6 %all-to-all-start.7 = ((bf16[16,64,256]{2,1,0:T(8,128)(2,1)}), bf16[16,64,256]{2,1,0:T(8,128)(2,1)S(1)}, u32[]{:S(2)}, u32[]{:S(2)}) async-start(bf16[16,64,256]{2,1,0:T(8,128)(2,1)} %broadcast_in_dim.196), calls=%async_computation.7 | async-start | bytes 1048576 | tf_op jit(solution)/shard_map/all_to_all | solution.py:31
  212.6 2.5 fusion.12
  216.4 5.5 %all-to-all-start.8 = ((bf16[16,3,64,128]{3,2,1,0:T(8,128)(2,1)}), bf16[16,3,64,128]{3,2,1,0:T(8,128)(2,1)S(1)}, u32[]{:S(2)}, u32[]{:S(2)}) async-start(bf16[16,3,64,128]{3,2,1,0:T(8,128)(2,1)} %broadcast_in_dim.197), calls=%async_computation.8 | async-start | bytes 1572864 | tf_op jit(solution)/shard_map/all_to_all | solution.py:31
  223.8 3.8 %collective-permute-start.54 = (bf16[256,256]{1,0:T(8,128)(2,1)}, bf16[256,256]{1,0:T(8,128)(2,1)S(1)}, u32[]{:S(2)}, u32[]{:S(2)}) collective-permute-start(bf16[256,256]{1,0:T(8,128)(2,1)} %collective-permute-done.53), channel_id=1, source_target_pairs={{0,240},{16,0},{32,16},{48,32},{64,48},{80,64},{96,80},{112,96},{1... | collective-permute-start | bytes 393224 | tf_op jit(solution)/shard_map/ppermute | solution.py:18
  227.8 2.6 collective-permute-start.27
  230.7 1.9 collective-permute-done.40
  234.0 2.6 collective-permute-start.28
  238.0 1.8 collective-permute-start.42
  239.9 2.3 collective-permute-start.29
  245.7 6.6 %all-to-all-start.9 = ((bf16[16,64,256]{2,1,0:T(8,128)(2,1)}), bf16[16,64,256]{2,1,0:T(8,128)(2,1)S(1)}, u32[]{:S(2)}, u32[]{:S(2)}) async-start(bf16[16,64,256]{2,1,0:T(8,128)(2,1)} %broadcast_in_dim.202), calls=%async_computation.9 | async-start | bytes 1048576 | tf_op jit(solution)/shard_map/all_to_all | solution.py:31
  259.4 2.9 all-to-all-done.9
  262.4 2.5 fusion.14
  266.0 3.7 %all-to-all-start.10 = ((bf16[16,2,64,128]{3,2,1,0:T(8,128)(2,1)}), bf16[16,2,64,128]{3,2,1,0:T(8,128)(2,1)S(1)}, u32[]{:S(2)}, u32[]{:S(2)}) async-start(bf16[16,2,64,128]{3,2,1,0:T(8,128)(2,1)} %broadcast_in_dim.203), calls=%async_computation.10 | async-start | bytes 1048576 | tf_op jit(solution)/shard_map/all_to_all | solution.py:31
  270.4 2.4 collective-permute-start.57
  275.8 1.7 collective-permute-done.43
  277.5 1.7 collective-permute-start.44
  283.5 6.6 %all-to-all-start.11 = ((bf16[16,64,256]{2,1,0:T(8,128)(2,1)}), bf16[16,64,256]{2,1,0:T(8,128)(2,1)S(1)}, u32[]{:S(2)}, u32[]{:S(2)}) async-start(bf16[16,64,256]{2,1,0:T(8,128)(2,1)} %broadcast_in_dim.208), calls=%async_computation.11 | async-start | bytes 1048576 | tf_op jit(solution)/shard_map/all_to_all | solution.py:31
  293.6 6.7 %all-to-all-done.11 = bf16[16,64,256]{2,1,0:T(8,128)(2,1)S(1)} async-done(((bf16[16,64,256]{2,1,0:T(8,128)(2,1)}), bf16[16,64,256]{2,1,0:T(8,128)(2,1)S(1)}, u32[]{:S(2)}, u32[]{:S(2)}) %all-to-all-start.11) | async-done | bytes 524320 | tf_op jit(solution)/shard_map/all_to_all | solution.py:31
  300.3 2.5 fusion.16
  303.7 3.5 %all-to-all-start.12 = ((bf16[16,1,64,128]{3,2,1,0:T(8,128)(2,1)}), bf16[16,1,64,128]{3,2,1,0:T(8,128)(2,1)S(1)}, u32[]{:S(2)}, u32[]{:S(2)}) async-start(bf16[16,1,64,128]{3,2,1,0:T(8,128)(2,1)} %broadcast_in_dim.210), calls=%async_computation.12 | async-start | bytes 524288 | tf_op jit(solution)/shard_map/all_to_all | solution.py:31
  307.3 2.4 collective-permute-start.59
  311.9 2.8 all-to-all-done.12
  315.8 4.0 %all-to-all-start.13 = ((bf16[16,64,256]{2,1,0:T(8,128)(2,1)}), bf16[16,64,256]{2,1,0:T(8,128)(2,1)S(1)}, u32[]{:S(2)}, u32[]{:S(2)}) async-start(bf16[16,64,256]{2,1,0:T(8,128)(2,1)} %broadcast_in_dim.214), calls=%async_computation.13 | async-start | bytes 1048576 | tf_op jit(solution)/shard_map/all_to_all | solution.py:31
  323.2 5.6 %all-to-all-done.13 = bf16[16,64,256]{2,1,0:T(8,128)(2,1)S(1)} async-done(((bf16[16,64,256]{2,1,0:T(8,128)(2,1)}), bf16[16,64,256]{2,1,0:T(8,128)(2,1)S(1)}, u32[]{:S(2)}, u32[]{:S(2)}) %all-to-all-start.13) | async-done | bytes 524320 | tf_op jit(solution)/shard_map/all_to_all | solution.py:31
  328.9 2.5 fusion.28
  (336 shorter events, 115.7 us)
Async XLA Ops:
  6.5 79.7 %all-gather.9.cloned.1.call-start = ((), (), s32[]{:S(2)}) async-start(), calls=%async_computation.14 | async-start | bytes 2228224 | tf_op jit(solution)/shard_map/all_gather | solution.py:70
  8.5 122.3 %all-gather.11.cloned.1.call-start = ((), (), s32[]{:S(2)}) async-start(), calls=%async_computation.15 | async-start | bytes 2228224 | tf_op jit(solution)/shard_map/all_gather | solution.py:70
  9.3 159.1 %all-gather.13.cloned.1.call-start = ((), (), s32[]{:S(2)}) async-start(), calls=%async_computation.16 | async-start | bytes 2228224 | tf_op jit(solution)/shard_map/all_gather | solution.py:70
  14.9 20.6 %collective-permute-start = (bf16[256,256]{1,0:T(8,128)(2,1)S(1)}, bf16[256,256]{1,0:T(8,128)(2,1)S(1)}, u32[]{:S(2)}, u32[]{:S(2)}) collective-permute-start(bf16[256,256]{1,0:T(8,128)(2,1)S(1)} %get-tuple-element.150), channel_id=1, source_target_pairs={{0,16},{16,32},{32,48},{48,64},{64,80},{80,96},{96,112},{112,128},... | collective-permute-start | bytes 393224 | tf_op jit(solution)/shard_map/ppermute | solution.py:16
  14.9 23.7 %collective-permute-start.8 = (bf16[256,256]{1,0:T(8,128)(2,1)S(1)}, bf16[256,256]{1,0:T(8,128)(2,1)S(1)}, u32[]{:S(2)}, u32[]{:S(2)}) collective-permute-start(bf16[256,256]{1,0:T(8,128)(2,1)S(1)} %get-tuple-element.150), channel_id=1, source_target_pairs={{0,240},{16,0},{32,16},{48,32},{64,48},{80,64},{96,80},{112,96},{1... | collective-permute-start | bytes 393224 | tf_op jit(solution)/shard_map/ppermute | solution.py:18
  15.4 12.4 %collective-permute-start.30 = (bf16[256,256]{1,0:T(8,128)(2,1)S(1)}, bf16[256,256]{1,0:T(8,128)(2,1)S(1)}, u32[]{:S(2)}, u32[]{:S(2)}) collective-permute-start(bf16[256,256]{1,0:T(8,128)(2,1)S(1)} %get-tuple-element.151), channel_id=1, source_target_pairs={{0,16},{16,32},{32,48},{48,64},{64,80},{80,96},{96,112},{112,128},... | collective-permute-start | bytes 393224 | tf_op jit(solution)/shard_map/ppermute | solution.py:16
  16.9 15.0 %collective-permute-start.45 = (bf16[256,256]{1,0:T(8,128)(2,1)S(1)}, bf16[256,256]{1,0:T(8,128)(2,1)S(1)}, u32[]{:S(2)}, u32[]{:S(2)}) collective-permute-start(bf16[256,256]{1,0:T(8,128)(2,1)S(1)} %get-tuple-element.148), channel_id=1, source_target_pairs={{0,16},{16,32},{32,48},{48,64},{64,80},{80,96},{96,112},{112,128},... | collective-permute-start | bytes 393224 | tf_op jit(solution)/shard_map/ppermute | solution.py:16
  17.4 10.7 %collective-permute-start.16 = (bf16[256,256]{1,0:T(8,128)(2,1)S(1)}, bf16[256,256]{1,0:T(8,128)(2,1)S(1)}, u32[]{:S(2)}, u32[]{:S(2)}) collective-permute-start(bf16[256,256]{1,0:T(8,128)(2,1)S(1)} %collective-permute-done.15), channel_id=1, source_target_pairs={{0,16},{16,32},{32,48},{48,64},{64,80},{80,96},{96,112},{112,128},... | collective-permute-start | bytes 393224 | tf_op jit(solution)/shard_map/ppermute | solution.py:16
  20.4 50.8 %all-to-all-start = ((bf16[16,64,256]{2,1,0:T(8,128)(2,1)}), bf16[16,64,256]{2,1,0:T(8,128)(2,1)S(1)}, u32[]{:S(2)}, u32[]{:S(2)}) async-start(bf16[16,64,256]{2,1,0:T(8,128)(2,1)} %broadcast_in_dim.83), calls=%async_computation | async-start | bytes 1048576 | tf_op jit(solution)/shard_map/all_to_all | solution.py:31
  27.2 169.6 %all-gather.15.cloned.1.call-start = ((), (), s32[]{:S(2)}) async-start(), calls=%async_computation.17 | async-start | bytes 2228224 | tf_op jit(solution)/shard_map/all_gather | solution.py:70
  28.2 6.8 %collective-permute-start.17 = (bf16[256,256]{1,0:T(8,128)(2,1)S(1)}, bf16[256,256]{1,0:T(8,128)(2,1)S(1)}, u32[]{:S(2)}, u32[]{:S(2)}) collective-permute-start(bf16[256,256]{1,0:T(8,128)(2,1)S(1)} %collective-permute-done.16), channel_id=1, source_target_pairs={{0,16},{16,32},{32,48},{48,64},{64,80},{80,96},{96,112},{112,128},... | collective-permute-start | bytes 393224 | tf_op jit(solution)/shard_map/ppermute | solution.py:16
  31.9 6.7 %collective-permute-start.46 = (bf16[256,256]{1,0:T(8,128)(2,1)S(1)}, bf16[256,256]{1,0:T(8,128)(2,1)S(1)}, u32[]{:S(2)}, u32[]{:S(2)}) collective-permute-start(bf16[256,256]{1,0:T(8,128)(2,1)S(1)} %collective-permute-done.45), channel_id=1, source_target_pairs={{0,16},{16,32},{32,48},{48,64},{64,80},{80,96},{96,112},{112,128},... | collective-permute-start | bytes 393224 | tf_op jit(solution)/shard_map/ppermute | solution.py:16
  35.5 6.6 %collective-permute-start.23 = (bf16[256,256]{1,0:T(8,128)(2,1)}, bf16[256,256]{1,0:T(8,128)(2,1)S(1)}, u32[]{:S(2)}, u32[]{:S(2)}) collective-permute-start(bf16[256,256]{1,0:T(8,128)(2,1)} %get-tuple-element.149), channel_id=1, source_target_pairs={{0,240},{16,0},{32,16},{48,32},{64,48},{80,64},{96,80},{112,96},{1... | collective-permute-start | bytes 393224 | tf_op jit(solution)/shard_map/ppermute | solution.py:18
  38.8 7.9 %collective-permute-start.33 = (bf16[256,256]{1,0:T(8,128)(2,1)}, bf16[256,256]{1,0:T(8,128)(2,1)S(1)}, u32[]{:S(2)}, u32[]{:S(2)}) collective-permute-start(bf16[256,256]{1,0:T(8,128)(2,1)} %collective-permute-done.32), channel_id=1, source_target_pairs={{0,16},{16,32},{32,48},{48,64},{64,80},{80,96},{96,112},{112,128},... | collective-permute-start | bytes 393224 | tf_op jit(solution)/shard_map/ppermute | solution.py:16
  40.5 8.5 %collective-permute-start.19 = (bf16[256,256]{1,0:T(8,128)(2,1)S(1)}, bf16[256,256]{1,0:T(8,128)(2,1)S(1)}, u32[]{:S(2)}, u32[]{:S(2)}) collective-permute-start(bf16[256,256]{1,0:T(8,128)(2,1)S(1)} %collective-permute-done.18), channel_id=1, source_target_pairs={{0,16},{16,32},{32,48},{48,64},{64,80},{80,96},{96,112},{112,128},... | collective-permute-start | bytes 393224 | tf_op jit(solution)/shard_map/ppermute | solution.py:16
  42.1 8.4 %collective-permute-start.9 = (bf16[256,256]{1,0:T(8,128)(2,1)S(1)}, bf16[256,256]{1,0:T(8,128)(2,1)S(1)}, u32[]{:S(2)}, u32[]{:S(2)}) collective-permute-start(bf16[256,256]{1,0:T(8,128)(2,1)S(1)} %collective-permute-done.8), channel_id=1, source_target_pairs={{0,240},{16,0},{32,16},{48,32},{64,48},{80,64},{96,80},{112,96},{1... | collective-permute-start | bytes 393224 | tf_op jit(solution)/shard_map/ppermute | solution.py:18
  44.4 10.5 %collective-permute-start.2 = (bf16[256,256]{1,0:T(8,128)(2,1)S(1)}, bf16[256,256]{1,0:T(8,128)(2,1)}, u32[]{:S(2)}, u32[]{:S(2)}) collective-permute-start(bf16[256,256]{1,0:T(8,128)(2,1)S(1)} %collective-permute-done.1), channel_id=1, source_target_pairs={{0,16},{16,32},{32,48},{48,64},{64,80},{80,96},{96,112},{112,128},... | collective-permute-start | bytes 393224 | tf_op jit(solution)/shard_map/ppermute | solution.py:16
  44.4 10.5 %collective-permute-start.48 = (bf16[256,256]{1,0:T(8,128)(2,1)S(1)}, bf16[256,256]{1,0:T(8,128)(2,1)S(1)}, u32[]{:S(2)}, u32[]{:S(2)}) collective-permute-start(bf16[256,256]{1,0:T(8,128)(2,1)S(1)} %collective-permute-done.47), channel_id=1, source_target_pairs={{0,16},{16,32},{32,48},{48,64},{64,80},{80,96},{96,112},{112,128},... | collective-permute-start | bytes 393224 | tf_op jit(solution)/shard_map/ppermute | solution.py:16
  46.6 8.4 %collective-permute-start.34 = (bf16[256,256]{1,0:T(8,128)(2,1)S(1)}, bf16[256,256]{1,0:T(8,128)(2,1)}, u32[]{:S(2)}, u32[]{:S(2)}) collective-permute-start(bf16[256,256]{1,0:T(8,128)(2,1)S(1)} %collective-permute-done.33), channel_id=1, source_target_pairs={{0,16},{16,32},{32,48},{48,64},{64,80},{80,96},{96,112},{112,128},... | collective-permute-start | bytes 393224 | tf_op jit(solution)/shard_map/ppermute | solution.py:16
  49.0 7.4 %collective-permute-start.20 = (bf16[256,256]{1,0:T(8,128)(2,1)S(1)}, bf16[256,256]{1,0:T(8,128)(2,1)S(1)}, u32[]{:S(2)}, u32[]{:S(2)}) collective-permute-start(bf16[256,256]{1,0:T(8,128)(2,1)S(1)} %collective-permute-done.19), channel_id=1, source_target_pairs={{0,16},{16,32},{32,48},{48,64},{64,80},{80,96},{96,112},{112,128},... | collective-permute-start | bytes 393224 | tf_op jit(solution)/shard_map/ppermute | solution.py:16
  50.5 8.4 %collective-permute-start.10 = (bf16[256,256]{1,0:T(8,128)(2,1)S(1)}, bf16[256,256]{1,0:T(8,128)(2,1)}, u32[]{:S(2)}, u32[]{:S(2)}) collective-permute-start(bf16[256,256]{1,0:T(8,128)(2,1)S(1)} %collective-permute-done.9), channel_id=1, source_target_pairs={{0,240},{16,0},{32,16},{48,32},{64,48},{80,64},{96,80},{112,96},{1... | collective-permute-start | bytes 393224 | tf_op jit(solution)/shard_map/ppermute | solution.py:18
  55.0 6.2 %collective-permute-start.3 = (bf16[256,256]{1,0:T(8,128)(2,1)}, bf16[256,256]{1,0:T(8,128)(2,1)}, u32[]{:S(2)}, u32[]{:S(2)}) collective-permute-start(bf16[256,256]{1,0:T(8,128)(2,1)} %collective-permute-done.2), channel_id=1, source_target_pairs={{0,16},{16,32},{32,48},{48,64},{64,80},{80,96},{96,112},{112,128},... | collective-permute-start | bytes 393224 | tf_op jit(solution)/shard_map/ppermute | solution.py:16
  55.0 6.2 %collective-permute-start.35 = (bf16[256,256]{1,0:T(8,128)(2,1)}, bf16[256,256]{1,0:T(8,128)(2,1)}, u32[]{:S(2)}, u32[]{:S(2)}) collective-permute-start(bf16[256,256]{1,0:T(8,128)(2,1)} %collective-permute-done.34), channel_id=1, source_target_pairs={{0,16},{16,32},{32,48},{48,64},{64,80},{80,96},{96,112},{112,128},... | collective-permute-start | bytes 393224 | tf_op jit(solution)/shard_map/ppermute | solution.py:16
  56.4 6.8 %collective-permute-start.21 = (bf16[256,256]{1,0:T(8,128)(2,1)S(1)}, bf16[256,256]{1,0:T(8,128)(2,1)}, u32[]{:S(2)}, u32[]{:S(2)}) collective-permute-start(bf16[256,256]{1,0:T(8,128)(2,1)S(1)} %collective-permute-done.20), channel_id=1, source_target_pairs={{0,16},{16,32},{32,48},{48,64},{64,80},{80,96},{96,112},{112,128},... | collective-permute-start | bytes 393224 | tf_op jit(solution)/shard_map/ppermute | solution.py:16
  58.8 12.4 %collective-permute-start.11 = (bf16[256,256]{1,0:T(8,128)(2,1)}, bf16[256,256]{1,0:T(8,128)(2,1)}, u32[]{:S(2)}, u32[]{:S(2)}) collective-permute-start(bf16[256,256]{1,0:T(8,128)(2,1)} %collective-permute-done.10), channel_id=1, source_target_pairs={{0,240},{16,0},{32,16},{48,32},{64,48},{80,64},{96,80},{112,96},{1... | collective-permute-start | bytes 393224 | tf_op jit(solution)/shard_map/ppermute | solution.py:18
  61.2 14.2 %collective-permute-start.4 = (bf16[256,256]{1,0:T(8,128)(2,1)}, bf16[256,256]{1,0:T(8,128)(2,1)}, u32[]{:S(2)}, u32[]{:S(2)}) collective-permute-start(bf16[256,256]{1,0:T(8,128)(2,1)} %collective-permute-done.3), channel_id=1, source_target_pairs={{0,16},{16,32},{32,48},{48,64},{64,80},{80,96},{96,112},{112,128},... | collective-permute-start | bytes 393224 | tf_op jit(solution)/shard_map/ppermute | solution.py:16
  61.2 17.1 %collective-permute-start.50 = (bf16[256,256]{1,0:T(8,128)(2,1)}, bf16[256,256]{1,0:T(8,128)(2,1)}, u32[]{:S(2)}, u32[]{:S(2)}) collective-permute-start(bf16[256,256]{1,0:T(8,128)(2,1)} %collective-permute-done.49), channel_id=1, source_target_pairs={{0,16},{16,32},{32,48},{48,64},{64,80},{80,96},{96,112},{112,128},... | collective-permute-start | bytes 393224 | tf_op jit(solution)/shard_map/ppermute | solution.py:16
  61.3 17.1 %collective-permute-start.36 = (bf16[256,256]{1,0:T(8,128)(2,1)}, bf16[256,256]{1,0:T(8,128)(2,1)}, u32[]{:S(2)}, u32[]{:S(2)}) collective-permute-start(bf16[256,256]{1,0:T(8,128)(2,1)} %collective-permute-done.35), channel_id=1, source_target_pairs={{0,16},{16,32},{32,48},{48,64},{64,80},{80,96},{96,112},{112,128},... | collective-permute-start | bytes 393224 | tf_op jit(solution)/shard_map/ppermute | solution.py:16
  63.2 15.2 %collective-permute-start.22 = (bf16[256,256]{1,0:T(8,128)(2,1)}, bf16[256,256]{1,0:T(8,128)(2,1)}, u32[]{:S(2)}, u32[]{:S(2)}) collective-permute-start(bf16[256,256]{1,0:T(8,128)(2,1)} %collective-permute-done.21), channel_id=1, source_target_pairs={{0,16},{16,32},{32,48},{48,64},{64,80},{80,96},{96,112},{112,128},... | collective-permute-start | bytes 393224 | tf_op jit(solution)/shard_map/ppermute | solution.py:16
  71.3 26.9 %collective-permute-start.24 = (bf16[256,256]{1,0:T(8,128)(2,1)S(1)}, bf16[256,256]{1,0:T(8,128)(2,1)}, u32[]{:S(2)}, u32[]{:S(2)}) collective-permute-start(bf16[256,256]{1,0:T(8,128)(2,1)S(1)} %collective-permute-done.23), channel_id=1, source_target_pairs={{0,240},{16,0},{32,16},{48,32},{64,48},{80,64},{96,80},{112,96},{1... | collective-permute-start | bytes 393224 | tf_op jit(solution)/shard_map/ppermute | solution.py:18
  75.4 23.5 %collective-permute-start.12 = (bf16[256,256]{1,0:T(8,128)(2,1)}, bf16[256,256]{1,0:T(8,128)(2,1)}, u32[]{:S(2)}, u32[]{:S(2)}) collective-permute-start(bf16[256,256]{1,0:T(8,128)(2,1)} %collective-permute-done.11), channel_id=1, source_target_pairs={{0,240},{16,0},{32,16},{48,32},{64,48},{80,64},{96,80},{112,96},{1... | collective-permute-start | bytes 393224 | tf_op jit(solution)/shard_map/ppermute | solution.py:18
  78.4 23.2 %collective-permute-start.5 = (bf16[256,256]{1,0:T(8,128)(2,1)}, bf16[256,256]{1,0:T(8,128)(2,1)}, u32[]{:S(2)}, u32[]{:S(2)}) collective-permute-start(bf16[256,256]{1,0:T(8,128)(2,1)} %collective-permute-done.4), channel_id=1, source_target_pairs={{0,16},{16,32},{32,48},{48,64},{64,80},{80,96},{96,112},{112,128},... | collective-permute-start | bytes 393224 | tf_op jit(solution)/shard_map/ppermute | solution.py:16
  78.4 24.0 %collective-permute-start.51 = (bf16[256,256]{1,0:T(8,128)(2,1)}, bf16[256,256]{1,0:T(8,128)(2,1)}, u32[]{:S(2)}, u32[]{:S(2)}) collective-permute-start(bf16[256,256]{1,0:T(8,128)(2,1)} %collective-permute-done.50), channel_id=1, source_target_pairs={{0,16},{16,32},{32,48},{48,64},{64,80},{80,96},{96,112},{112,128},... | collective-permute-start | bytes 393224 | tf_op jit(solution)/shard_map/ppermute | solution.py:16
  78.4 25.0 %collective-permute-start.37 = (bf16[256,256]{1,0:T(8,128)(2,1)}, bf16[256,256]{1,0:T(8,128)(2,1)}, u32[]{:S(2)}, u32[]{:S(2)}) collective-permute-start(bf16[256,256]{1,0:T(8,128)(2,1)} %collective-permute-done.36), channel_id=1, source_target_pairs={{0,16},{16,32},{32,48},{48,64},{64,80},{80,96},{96,112},{112,128},... | collective-permute-start | bytes 393224 | tf_op jit(solution)/shard_map/ppermute | solution.py:16
  89.9 20.5 %all-to-all-start.1 = ((bf16[16,3,64,128]{3,2,1,0:T(8,128)(2,1)}), bf16[16,3,64,128]{3,2,1,0:T(8,128)(2,1)S(1)}, u32[]{:S(2)}, u32[]{:S(2)}) async-start(bf16[16,3,64,128]{3,2,1,0:T(8,128)(2,1)} %broadcast_in_dim.85), calls=%async_computation.1 | async-start | bytes 1572864 | tf_op jit(solution)/shard_map/all_to_all | solution.py:31
  98.2 23.9 %collective-permute-start.38 = (bf16[256,256]{1,0:T(8,128)(2,1)}, bf16[256,256]{1,0:T(8,128)(2,1)}, u32[]{:S(2)}, u32[]{:S(2)}) collective-permute-start(bf16[256,256]{1,0:T(8,128)(2,1)} %copy-done.39), channel_id=1, source_target_pairs={{0,240},{16,0},{32,16},{48,32},{64,48},{80,64},{96,80},{112,96},{1... | collective-permute-start | bytes 393224 | tf_op jit(solution)/shard_map/ppermute | solution.py:18
  98.9 23.9 %collective-permute-start.25 = (bf16[256,256]{1,0:T(8,128)(2,1)}, bf16[256,256]{1,0:T(8,128)(2,1)}, u32[]{:S(2)}, u32[]{:S(2)}) collective-permute-start(bf16[256,256]{1,0:T(8,128)(2,1)} %collective-permute-done.24), channel_id=1, source_target_pairs={{0,240},{16,0},{32,16},{48,32},{64,48},{80,64},{96,80},{112,96},{1... | collective-permute-start | bytes 393224 | tf_op jit(solution)/shard_map/ppermute | solution.py:18
  101.6 23.5 %collective-permute-start.13 = (bf16[256,256]{1,0:T(8,128)(2,1)}, bf16[256,256]{1,0:T(8,128)(2,1)}, u32[]{:S(2)}, u32[]{:S(2)}) collective-permute-start(bf16[256,256]{1,0:T(8,128)(2,1)} %collective-permute-done.12), channel_id=1, source_target_pairs={{0,240},{16,0},{32,16},{48,32},{64,48},{80,64},{96,80},{112,96},{1... | collective-permute-start | bytes 393224 | tf_op jit(solution)/shard_map/ppermute | solution.py:18
  102.4 23.5 %collective-permute-start.6 = (bf16[256,256]{1,0:T(8,128)(2,1)}, bf16[256,256]{1,0:T(8,128)(2,1)}, u32[]{:S(2)}, u32[]{:S(2)}) collective-permute-start(bf16[256,256]{1,0:T(8,128)(2,1)} %collective-permute-done.5), channel_id=1, source_target_pairs={{0,16},{16,32},{32,48},{48,64},{64,80},{80,96},{96,112},{112,128},... | collective-permute-start | bytes 393224 | tf_op jit(solution)/shard_map/ppermute | solution.py:16
  103.4 22.6 %collective-permute-start.52 = (bf16[256,256]{1,0:T(8,128)(2,1)}, bf16[256,256]{1,0:T(8,128)(2,1)}, u32[]{:S(2)}, u32[]{:S(2)}) collective-permute-start(bf16[256,256]{1,0:T(8,128)(2,1)} %collective-permute-done.51), channel_id=1, source_target_pairs={{0,16},{16,32},{32,48},{48,64},{64,80},{80,96},{96,112},{112,128},... | collective-permute-start | bytes 393224 | tf_op jit(solution)/shard_map/ppermute | solution.py:16
  111.6 19.2 %all-to-all-start.2 = ((bf16[16,64,256]{2,1,0:T(8,128)(2,1)}), bf16[16,64,256]{2,1,0:T(8,128)(2,1)S(1)}, u32[]{:S(2)}, u32[]{:S(2)}) async-start(bf16[16,64,256]{2,1,0:T(8,128)(2,1)} %broadcast_in_dim.89), calls=%async_computation.2 | async-start | bytes 1048576 | tf_op jit(solution)/shard_map/all_to_all | solution.py:31
  122.1 101.7 %collective-permute-start.53 = (bf16[256,256]{1,0:T(8,128)(2,1)}, bf16[256,256]{1,0:T(8,128)(2,1)}, u32[]{:S(2)}, u32[]{:S(2)}) collective-permute-start(bf16[256,256]{1,0:T(8,128)(2,1)} %copy-done.38), channel_id=1, source_target_pairs={{0,240},{16,0},{32,16},{48,32},{64,48},{80,64},{96,80},{112,96},{1... | collective-permute-start | bytes 393224 | tf_op jit(solution)/shard_map/ppermute | solution.py:18
  122.9 104.8 %collective-permute-start.39 = (bf16[256,256]{1,0:T(8,128)(2,1)}, bf16[256,256]{1,0:T(8,128)(2,1)}, u32[]{:S(2)}, u32[]{:S(2)}) collective-permute-start(bf16[256,256]{1,0:T(8,128)(2,1)} %collective-permute-done.38), channel_id=1, source_target_pairs={{0,240},{16,0},{32,16},{48,32},{64,48},{80,64},{96,80},{112,96},{1... | collective-permute-start | bytes 393224 | tf_op jit(solution)/shard_map/ppermute | solution.py:18
  125.1 102.7 %collective-permute-start.26 = (bf16[256,256]{1,0:T(8,128)(2,1)}, bf16[256,256]{1,0:T(8,128)(2,1)}, u32[]{:S(2)}, u32[]{:S(2)}) collective-permute-start(bf16[256,256]{1,0:T(8,128)(2,1)} %collective-permute-done.25), channel_id=1, source_target_pairs={{0,240},{16,0},{32,16},{48,32},{64,48},{80,64},{96,80},{112,96},{1... | collective-permute-start | bytes 393224 | tf_op jit(solution)/shard_map/ppermute | solution.py:18
  125.9 84.1 %collective-permute-start.14 = (bf16[256,256]{1,0:T(8,128)(2,1)}, bf16[256,256]{1,0:T(8,128)(2,1)}, u32[]{:S(2)}, u32[]{:S(2)}) collective-permute-start(bf16[256,256]{1,0:T(8,128)(2,1)} %collective-permute-done.13), channel_id=1, source_target_pairs={{0,240},{16,0},{32,16},{48,32},{64,48},{80,64},{96,80},{112,96},{1... | collective-permute-start | bytes 393224 | tf_op jit(solution)/shard_map/ppermute | solution.py:18
  125.9 32.1 %collective-permute-start.7 = (bf16[256,256]{1,0:T(8,128)(2,1)}, bf16[256,256]{1,0:T(8,128)(2,1)}, u32[]{:S(2)}, u32[]{:S(2)}) collective-permute-start(bf16[256,256]{1,0:T(8,128)(2,1)} %collective-permute-done.6), channel_id=1, source_target_pairs={{0,16},{16,32},{32,48},{48,64},{64,80},{80,96},{96,112},{112,128},... | collective-permute-start | bytes 393224 | tf_op jit(solution)/shard_map/ppermute | solution.py:16
  134.3 18.3 %all-to-all-start.3 = ((bf16[16,2,64,128]{3,2,1,0:T(8,128)(2,1)}), bf16[16,2,64,128]{3,2,1,0:T(8,128)(2,1)S(1)}, u32[]{:S(2)}, u32[]{:S(2)}) async-start(bf16[16,2,64,128]{3,2,1,0:T(8,128)(2,1)} %broadcast_in_dim.91), calls=%async_computation.3 | async-start | bytes 1048576 | tf_op jit(solution)/shard_map/all_to_all | solution.py:31
  153.7 14.6 %all-to-all-start.4 = ((bf16[16,64,256]{2,1,0:T(8,128)(2,1)}), bf16[16,64,256]{2,1,0:T(8,128)(2,1)S(1)}, u32[]{:S(2)}, u32[]{:S(2)}) async-start(bf16[16,64,256]{2,1,0:T(8,128)(2,1)} %broadcast_in_dim.187), calls=%async_computation.4 | async-start | bytes 1048576 | tf_op jit(solution)/shard_map/all_to_all | solution.py:31
  171.7 11.1 %all-to-all-start.5 = ((bf16[16,1,64,128]{3,2,1,0:T(8,128)(2,1)}), bf16[16,1,64,128]{3,2,1,0:T(8,128)(2,1)S(1)}, u32[]{:S(2)}, u32[]{:S(2)}) async-start(bf16[16,1,64,128]{3,2,1,0:T(8,128)(2,1)} %broadcast_in_dim.191), calls=%async_computation.5 | async-start | bytes 524288 | tf_op jit(solution)/shard_map/all_to_all | solution.py:31
  183.9 12.9 %all-to-all-start.6 = ((bf16[16,64,256]{2,1,0:T(8,128)(2,1)}), bf16[16,64,256]{2,1,0:T(8,128)(2,1)S(1)}, u32[]{:S(2)}, u32[]{:S(2)}) async-start(bf16[16,64,256]{2,1,0:T(8,128)(2,1)} %broadcast_in_dim.195), calls=%async_computation.6 | async-start | bytes 1048576 | tf_op jit(solution)/shard_map/all_to_all | solution.py:31
  200.1 12.5 %all-to-all-start.7 = ((bf16[16,64,256]{2,1,0:T(8,128)(2,1)}), bf16[16,64,256]{2,1,0:T(8,128)(2,1)S(1)}, u32[]{:S(2)}, u32[]{:S(2)}) async-start(bf16[16,64,256]{2,1,0:T(8,128)(2,1)} %broadcast_in_dim.196), calls=%async_computation.7 | async-start | bytes 1048576 | tf_op jit(solution)/shard_map/all_to_all | solution.py:31
  216.4 28.0 %all-to-all-start.8 = ((bf16[16,3,64,128]{3,2,1,0:T(8,128)(2,1)}), bf16[16,3,64,128]{3,2,1,0:T(8,128)(2,1)S(1)}, u32[]{:S(2)}, u32[]{:S(2)}) async-start(bf16[16,3,64,128]{3,2,1,0:T(8,128)(2,1)} %broadcast_in_dim.197), calls=%async_computation.8 | async-start | bytes 1572864 | tf_op jit(solution)/shard_map/all_to_all | solution.py:31
  223.8 6.6 %collective-permute-start.54 = (bf16[256,256]{1,0:T(8,128)(2,1)}, bf16[256,256]{1,0:T(8,128)(2,1)S(1)}, u32[]{:S(2)}, u32[]{:S(2)}) collective-permute-start(bf16[256,256]{1,0:T(8,128)(2,1)} %collective-permute-done.53), channel_id=1, source_target_pairs={{0,240},{16,0},{32,16},{48,32},{64,48},{80,64},{96,80},{112,96},{1... | collective-permute-start | bytes 393224 | tf_op jit(solution)/shard_map/ppermute | solution.py:18
  236.6 33.8 %collective-permute-start.56 = (bf16[256,256]{1,0:T(8,128)(2,1)S(1)}, bf16[256,256]{1,0:T(8,128)(2,1)S(1)}, u32[]{:S(2)}, u32[]{:S(2)}) collective-permute-start(bf16[256,256]{1,0:T(8,128)(2,1)S(1)} %collective-permute-done.55), channel_id=1, source_target_pairs={{0,240},{16,0},{32,16},{48,32},{64,48},{80,64},{96,80},{112,96},{1... | collective-permute-start | bytes 393224 | tf_op jit(solution)/shard_map/ppermute | solution.py:18
  238.0 34.8 %collective-permute-start.42 = (bf16[256,256]{1,0:T(8,128)(2,1)S(1)}, bf16[256,256]{1,0:T(8,128)(2,1)S(1)}, u32[]{:S(2)}, u32[]{:S(2)}) collective-permute-start(bf16[256,256]{1,0:T(8,128)(2,1)S(1)} %collective-permute-done.41), channel_id=1, source_target_pairs={{0,240},{16,0},{32,16},{48,32},{64,48},{80,64},{96,80},{112,96},{1... | collective-permute-start | bytes 393224 | tf_op jit(solution)/shard_map/ppermute | solution.py:18
  239.9 18.0 %collective-permute-start.29 = (bf16[256,256]{1,0:T(8,128)(2,1)}, bf16[256,256]{1,0:T(8,128)(2,1)}, u32[]{:S(2)}, u32[]{:S(2)}) collective-permute-start(bf16[256,256]{1,0:T(8,128)(2,1)} %collective-permute-done.28), channel_id=1, source_target_pairs={{0,240},{16,0},{32,16},{48,32},{64,48},{80,64},{96,80},{112,96},{1... | collective-permute-start | bytes 393224 | tf_op jit(solution)/shard_map/ppermute | solution.py:18
  245.7 16.6 %all-to-all-start.9 = ((bf16[16,64,256]{2,1,0:T(8,128)(2,1)}), bf16[16,64,256]{2,1,0:T(8,128)(2,1)S(1)}, u32[]{:S(2)}, u32[]{:S(2)}) async-start(bf16[16,64,256]{2,1,0:T(8,128)(2,1)} %broadcast_in_dim.202), calls=%async_computation.9 | async-start | bytes 1048576 | tf_op jit(solution)/shard_map/all_to_all | solution.py:31
  266.0 16.4 %all-to-all-start.10 = ((bf16[16,2,64,128]{3,2,1,0:T(8,128)(2,1)}), bf16[16,2,64,128]{3,2,1,0:T(8,128)(2,1)S(1)}, u32[]{:S(2)}, u32[]{:S(2)}) async-start(bf16[16,2,64,128]{3,2,1,0:T(8,128)(2,1)} %broadcast_in_dim.203), calls=%async_computation.10 | async-start | bytes 1048576 | tf_op jit(solution)/shard_map/all_to_all | solution.py:31
  274.8 32.5 %collective-permute-start.58 = (bf16[256,256]{1,0:T(8,128)(2,1)S(1)}, bf16[256,256]{1,0:T(8,128)(2,1)S(1)}, u32[]{:S(2)}, u32[]{:S(2)}) collective-permute-start(bf16[256,256]{1,0:T(8,128)(2,1)S(1)} %collective-permute-done.57), channel_id=1, source_target_pairs={{0,240},{16,0},{32,16},{48,32},{64,48},{80,64},{96,80},{112,96},{1... | collective-permute-start | bytes 393224 | tf_op jit(solution)/shard_map/ppermute | solution.py:18
  277.5 15.4 %collective-permute-start.44 = (bf16[256,256]{1,0:T(8,128)(2,1)S(1)}, bf16[256,256]{1,0:T(8,128)(2,1)S(1)}, u32[]{:S(2)}, u32[]{:S(2)}) collective-permute-start(bf16[256,256]{1,0:T(8,128)(2,1)S(1)} %collective-permute-done.43), channel_id=1, source_target_pairs={{0,240},{16,0},{32,16},{48,32},{64,48},{80,64},{96,80},{112,96},{1... | collective-permute-start | bytes 393224 | tf_op jit(solution)/shard_map/ppermute | solution.py:18
  283.5 16.7 %all-to-all-start.11 = ((bf16[16,64,256]{2,1,0:T(8,128)(2,1)}), bf16[16,64,256]{2,1,0:T(8,128)(2,1)S(1)}, u32[]{:S(2)}, u32[]{:S(2)}) async-start(bf16[16,64,256]{2,1,0:T(8,128)(2,1)} %broadcast_in_dim.208), calls=%async_computation.11 | async-start | bytes 1048576 | tf_op jit(solution)/shard_map/all_to_all | solution.py:31
  303.7 11.0 %all-to-all-start.12 = ((bf16[16,1,64,128]{3,2,1,0:T(8,128)(2,1)}), bf16[16,1,64,128]{3,2,1,0:T(8,128)(2,1)S(1)}, u32[]{:S(2)}, u32[]{:S(2)}) async-start(bf16[16,1,64,128]{3,2,1,0:T(8,128)(2,1)} %broadcast_in_dim.210), calls=%async_computation.12 | async-start | bytes 524288 | tf_op jit(solution)/shard_map/all_to_all | solution.py:31
  307.3 15.3 %collective-permute-start.59 = (bf16[256,256]{1,0:T(8,128)(2,1)S(1)}, bf16[256,256]{1,0:T(8,128)(2,1)S(1)}, u32[]{:S(2)}, u32[]{:S(2)}) collective-permute-start(bf16[256,256]{1,0:T(8,128)(2,1)S(1)} %collective-permute-done.58), channel_id=1, source_target_pairs={{0,240},{16,0},{32,16},{48,32},{64,48},{80,64},{96,80},{112,96},{1... | collective-permute-start | bytes 393224 | tf_op jit(solution)/shard_map/ppermute | solution.py:18
  315.8 13.0 %all-to-all-start.13 = ((bf16[16,64,256]{2,1,0:T(8,128)(2,1)}), bf16[16,64,256]{2,1,0:T(8,128)(2,1)S(1)}, u32[]{:S(2)}, u32[]{:S(2)}) async-start(bf16[16,64,256]{2,1,0:T(8,128)(2,1)} %broadcast_in_dim.214), calls=%async_computation.13 | async-start | bytes 1048576 | tf_op jit(solution)/shard_map/all_to_all | solution.py:31
  (62 other events, 1009.1 us)
Sparse Core Ops, SparseCore 0:
  9.1 50.0 all-gather.8
  61.0 40.6 all-gather.10
  103.4 41.0 all-gather.12
  146.1 40.7 all-gather.14
